TPU v7x, 768 devices: a whole 4x8x12 slice. The times are simulated.
768 devices in a mesh: ctx: 384 (over x, z, y_lo, core), grp: 2 (over y_hi).
Axes of the slice: x: 4, y: 8 (y_hi: 2, y_lo: 4; y = y_hi * 4 + y_lo), z: 12, core: 2. Of those that a mesh axis runs over, the one named last changes fastest.
Arguments:
- doc_lengths: int32 [192], replicated, may hold values from 1 to 8192, 98304 in all
- query_raw: bfloat16 [98304, 2048], P(('ctx', 'grp')), may hold values from -40 to 40
- key_raw: bfloat16 [98304, 1024], P(('ctx', 'grp')), may hold values from -40 to 40
- value_matrix: bfloat16 [98304, 1024], P(('ctx', 'grp')), may hold values from -5 to 5
- out_grad: bfloat16 [98304, 2048], P(('ctx', 'grp')), may hold values from -5 to 5
- query_gain: float32 [128], replicated, may hold values from 0.5 to 6
- key_gain: float32 [128], replicated, may hold values from 0.5 to 6
Outputs:
- grad_query: bfloat16 [98304, 2048], P(('ctx', 'grp'))
- grad_key: bfloat16 [98304, 1024], P(('ctx', 'grp'))
- grad_value: bfloat16 [98304, 1024], P(('ctx', 'grp'))
- grad_query_gain: float32 [128], replicated
- grad_key_gain: float32 [128], replicated
Inputs may be any that keep to these rules, and one draw needn't show every extreme that they name: `doc_lengths`: lengths of the packed documents in order; they sum to 98304, and one of them is exactly 8192.
All inputs are finite; a program needn't handle non-finite values.
Results may differ from a plain program's by a relative error of at most 0.035.
The roundings to bfloat16 on the way count: a program that leaves them out, or rounds other values in their place, can miss the bound.
Values may be sent and summed in bfloat16 or wider, within the bound.
A program may use at most 64 MiB of HBM per device.

v0:
```python
import jax
import jax.numpy as jnp
from jax import lax
from jax.sharding import PartitionSpec as P

HEAD_SIZE = 128
WINDOW = 256


eps_norm = 1e-06
score_scale = 168.0 ** (-0.5)
rope_base = 10000.0
masked_score = -1e30


def from_behind(value, axis, steps):
    count = lax.axis_size(axis)
    initial, last = (max(0, -steps), min(count, count - steps))
    return lax.ppermute(value, axis, [(source, source + steps) for source in range(initial, last)])


def doc_places(token_ids, doc_lengths):
    doc_ends = jnp.cumsum(doc_lengths)
    before = doc_ends[None, :] <= token_ids[:, None]
    doc_ids = jnp.sum(before.astype(jnp.int32), axis=1)
    starts = jnp.max(jnp.where(before, doc_ends[None, :], 0), axis=1)
    return (doc_ids, token_ids - starts)


def rotary_tables(positions):
    half_width = HEAD_SIZE // 2
    frequency = rope_base ** (-2.0 * jnp.arange(half_width, dtype=jnp.float32) / HEAD_SIZE)
    angles = positions.astype(jnp.float32)[:, None] * frequency[None, :]
    return (jnp.cos(angles), jnp.sin(angles))


def norm_rotate(raw_rows, norm_gain, cosine, sine_table):
    row_count = raw_rows.shape[0]
    raw_values = raw_rows.astype(jnp.float32).reshape(row_count, -1, HEAD_SIZE)
    row_scale = lax.rsqrt(jnp.mean(raw_values * raw_values, axis=-1, keepdims=True) + eps_norm)
    normed = raw_values * row_scale * norm_gain
    front_half = normed[..., : HEAD_SIZE // 2]
    back_half = normed[..., HEAD_SIZE // 2 :]
    cos_rows = cosine[:, None, :]
    sin_rows = sine_table[:, None, :]
    rotated = jnp.concatenate(
        [
            front_half * cos_rows - back_half * sin_rows,
            back_half * cos_rows + front_half * sin_rows,
        ],
        -1,
    )
    return rotated.reshape(row_count, -1).astype(jnp.bfloat16)


def unrotate_norm(grad_rot, raw_rows, norm_gain, cosine, sine_table):
    row_count = grad_rot.shape[0]
    grad_rows = grad_rot.reshape(row_count, -1, HEAD_SIZE)
    front_half = grad_rows[..., : HEAD_SIZE // 2]
    back_half = grad_rows[..., HEAD_SIZE // 2 :]
    cos_rows = cosine[:, None, :]
    sin_rows = sine_table[:, None, :]
    grad_normed = jnp.concatenate(
        [
            front_half * cos_rows + back_half * sin_rows,
            back_half * cos_rows - front_half * sin_rows,
        ],
        -1,
    )
    raw_values = raw_rows.astype(jnp.float32).reshape(row_count, -1, HEAD_SIZE)
    row_scale = lax.rsqrt(jnp.mean(raw_values * raw_values, axis=-1, keepdims=True) + eps_norm)
    gain_grad = jnp.sum(grad_normed * raw_values * row_scale, axis=(0, 1))
    weighted = grad_normed * norm_gain
    raw_grad = row_scale * weighted - raw_values * row_scale**3 * jnp.mean(
        weighted * raw_values, axis=-1, keepdims=True
    )
    return (raw_grad.reshape(row_count, -1).astype(jnp.bfloat16), gain_grad)


def head_grads(queries, grads_out, key_block, value_block, visible):
    scores = (
        jnp.einsum("qhd,kd->hqk", queries, key_block, preferred_element_type=jnp.float32)
        * score_scale
    )
    scores = jnp.where(visible[None], scores, masked_score)
    row_top = jnp.max(scores, axis=-1, keepdims=True)
    exps_rows = jnp.exp(scores - row_top)
    weights = exps_rows / jnp.sum(exps_rows, axis=-1, keepdims=True)
    probs_low = weights.astype(jnp.bfloat16)
    prob_grad = jnp.einsum(
        "qhd,kd->hqk", grads_out, value_block, preferred_element_type=jnp.float32
    )
    row_delta = jnp.sum(weights * prob_grad, axis=-1, keepdims=True)
    score_grad = (weights * (prob_grad - row_delta)).astype(jnp.bfloat16)
    query_grad = (
        jnp.einsum("hqk,kd->qhd", score_grad, key_block, preferred_element_type=jnp.float32)
        * score_scale
    )
    key_grad = (
        jnp.einsum("hqk,qhd->kd", score_grad, queries, preferred_element_type=jnp.float32)
        * score_scale
    )
    value_grad = jnp.einsum("hqk,qhd->kd", probs_low, grads_out, preferred_element_type=jnp.float32)
    return (query_grad, key_grad, value_grad)


def on_device(doc_lengths, query_raw, key_raw, value_matrix, out_grad, query_gain, key_gain):
    tok_rows = query_raw.shape[0]
    halo_depth = WINDOW // tok_rows
    padding_rows = halo_depth * tok_rows
    key_count = padding_rows + tok_rows
    group_width = query_raw.shape[1] // key_raw.shape[1]
    device_at = lax.axis_index(("ctx", "grp"))
    key_tokens = (device_at - halo_depth) * tok_rows + jnp.arange(key_count, dtype=jnp.int32)
    key_docs, key_pos = doc_places(key_tokens, doc_lengths)
    key_cos, key_sin = rotary_tables(key_pos)
    own_tokens = key_tokens[padding_rows:]
    own_docs = key_docs[padding_rows:]
    own_cos = key_cos[padding_rows:]
    own_sin = key_sin[padding_rows:]
    own_key_rot = norm_rotate(key_raw, key_gain, own_cos, own_sin)
    received = []
    for hop_count in range(1, halo_depth + 1):
        received.append(from_behind((own_key_rot, value_matrix), ("ctx", "grp"), hop_count))
    ordered = received[::-1]
    far_keys = jnp.concatenate([pair_rows[0] for pair_rows in ordered], 0)
    far_values = jnp.concatenate([pair_rows[1] for pair_rows in ordered], 0)
    query_rot = norm_rotate(query_raw, query_gain, own_cos, own_sin)
    all_keys = jnp.concatenate([far_keys, own_key_rot], 0)
    all_values = jnp.concatenate([far_values, value_matrix], 0)
    same_doc = own_docs[:, None] == key_docs[None, :]
    causal = key_tokens[None, :] <= own_tokens[:, None]
    inside = own_tokens[:, None] - key_tokens[None, :] < WINDOW
    visible = same_doc & causal & inside & (key_tokens[None, :] >= 0)
    query_parts, key_parts, value_parts = ([], [], [])
    for key_value_head in range(key_raw.shape[1] // HEAD_SIZE):
        key_cols = slice(key_value_head * HEAD_SIZE, (key_value_head + 1) * HEAD_SIZE)
        query_cols = slice(
            key_value_head * group_width * HEAD_SIZE, (key_value_head + 1) * group_width * HEAD_SIZE
        )
        query_grad, key_grad, value_grad = head_grads(
            query_rot[:, query_cols].reshape(tok_rows, group_width, HEAD_SIZE),
            out_grad[:, query_cols].reshape(tok_rows, group_width, HEAD_SIZE),
            all_keys[:, key_cols],
            all_values[:, key_cols],
            visible,
        )
        query_parts.append(query_grad.reshape(tok_rows, group_width * HEAD_SIZE))
        key_parts.append(key_grad)
        value_parts.append(value_grad)
    query_term = jnp.concatenate(query_parts, 1)
    key_term = jnp.concatenate(key_parts, 1)
    value_term = jnp.concatenate(value_parts, 1)
    key_sum = key_term[padding_rows:]
    value_sum = value_term[padding_rows:]
    for hop_count in range(1, halo_depth + 1):
        row_start = (halo_depth - hop_count) * tok_rows
        outbound = (
            key_term[row_start : row_start + tok_rows].astype(jnp.bfloat16),
            value_term[row_start : row_start + tok_rows].astype(jnp.bfloat16),
        )
        inbound = from_behind((outbound[0], outbound[1]), ("ctx", "grp"), -hop_count)
        key_sum = key_sum + inbound[0].astype(jnp.float32)
        value_sum = value_sum + inbound[1].astype(jnp.float32)
    grad_query, query_gain_part = unrotate_norm(query_term, query_raw, query_gain, own_cos, own_sin)
    grad_key, key_gain_part = unrotate_norm(key_sum, key_raw, key_gain, own_cos, own_sin)
    grad_query_gain, grad_key_gain = lax.psum((query_gain_part, key_gain_part), ("ctx", "grp"))
    return (grad_query, grad_key, value_sum.astype(jnp.bfloat16), grad_query_gain, grad_key_gain)


def solution(mesh):
    placed = (
        P(),
        P(("ctx", "grp"), None),
        P(("ctx", "grp"), None),
        P(("ctx", "grp"), None),
        P(("ctx", "grp"), None),
        P(),
        P(),
    )
    return jax.shard_map(
        on_device,
        mesh=mesh,
        in_specs=placed,
        out_specs=(
            P(("ctx", "grp"), None),
            P(("ctx", "grp"), None),
            P(("ctx", "grp"), None),
            P(),
            P(),
        ),
        check_vma=False,
    )
```

profile of v0, /device:TPU:1, one launch (start us, length us, event | category | flops | bytes accessed | tf_op | source)
XLA Modules:
  0.0 282.3 jit_solution(16489279537875046687)
XLA Ops:
  6.1 4.6 %collective-permute-start = (bf16[128,1024]{1,0:T(8,128)(2,1)}, bf16[128,1024]{1,0:T(8,128)(2,1)}, u32[]{:S(2)}, u32[]{:S(2)}) collective-permute-start(bf16[128,1024]{1,0:T(8,128)(2,1)} %bitcast.531), channel_id=1, source_target_pairs={{0,2},{1,3},{2,4},{3,5},{4,6},{5,7},{6,8},{7,9},{8,10},{9,11},{10,... | collective-permute-start | bytes 786440 | tf_op jit(solution)/shard_map/ppermute | solution.py:19
  10.7 6.6 %collective-permute-start.1 = (bf16[128,1024]{1,0:T(8,128)(2,1)}, bf16[128,1024]{1,0:T(8,128)(2,1)}, u32[]{:S(2)}, u32[]{:S(2)}) collective-permute-start(bf16[128,1024]{1,0:T(8,128)(2,1)} %bitcast.531), channel_id=1, source_target_pairs={{0,1},{1,2},{2,3},{3,4},{4,5},{5,6},{6,7},{7,8},{8,9},{9,10},{10,1... | collective-permute-start | bytes 786440 | tf_op jit(solution)/shard_map/ppermute | solution.py:19
  17.3 2.2 collective-permute-start.2
  19.5 3.9 %collective-permute-start.3 = (bf16[128,1024]{1,0:T(8,128)(2,1)}, bf16[128,1024]{1,0:T(8,128)(2,1)}, u32[]{:S(2)}, u32[]{:S(2)}) collective-permute-start(bf16[128,1024]{1,0:T(8,128)(2,1)} %param.10), channel_id=1, source_target_pairs={{0,1},{1,2},{2,3},{3,4},{4,5},{5,6},{6,7},{7,8},{8,9},{9,10},{10,1... | collective-permute-start | bytes 786440 | tf_op jit(solution)/shard_map/ppermute | solution.py:19
  52.4 1.9 fusion.133
  58.5 2.1 fusion.47
  60.7 2.6 fusion.134
  63.2 2.5 fusion.135
  65.8 2.5 fusion.136
  68.3 2.6 fusion.137
  70.9 2.5 fusion.138
  73.4 1.9 fusion.139
  75.4 1.9 fusion.140
  96.6 1.8 fusion.59
  98.5 1.8 fusion.57
  102.1 1.8 fusion.53
  103.9 1.8 fusion.51
  105.7 1.8 fusion.49
  109.9 3.1 %collective-permute-start.5 = (bf16[128,1024]{0,1:T(8,128)(2,1)}, bf16[128,1024]{0,1:T(8,128)(2,1)}, u32[]{:S(2)}, u32[]{:S(2)}) collective-permute-start(bf16[128,1024]{0,1:T(8,128)(2,1)} %get-tuple-element.51), channel_id=1, source_target_pairs={{2,0},{3,1},{4,2},{5,3},{6,4},{7,5},{8,6},{9,7},{10,8},{11,9},{12,... | collective-permute-start | bytes 786440 | tf_op jit(solution)/shard_map/ppermute | solution.py:19
  113.1 4.0 %collective-permute-start.4 = (bf16[128,1024]{0,1:T(8,128)(2,1)}, bf16[128,1024]{0,1:T(8,128)(2,1)}, u32[]{:S(2)}, u32[]{:S(2)}) collective-permute-start(bf16[128,1024]{0,1:T(8,128)(2,1)} %get-tuple-element.50), channel_id=1, source_target_pairs={{1,0},{2,1},{3,2},{4,3},{5,4},{6,5},{7,6},{8,7},{9,8},{10,9},{11,1... | collective-permute-start | bytes 786440 | tf_op jit(solution)/shard_map/ppermute | solution.py:19
  117.1 2.1 fusion.46
  119.3 2.1 fusion.45
  121.4 2.1 fusion.44
  123.6 2.1 fusion.43
  125.8 2.1 fusion.42
  127.9 2.1 fusion.41
  130.0 2.1 fusion.40
  134.5 1.9 collective-permute-start.7
  136.4 4.4 %collective-permute-start.6 = (bf16[128,1024]{0,1:T(8,128)(2,1)}, bf16[128,1024]{0,1:T(8,128)(2,1)}, u32[]{:S(2)}, u32[]{:S(2)}) collective-permute-start(bf16[128,1024]{0,1:T(8,128)(2,1)} %get-tuple-element.48), channel_id=1, source_target_pairs={{1,0},{2,1},{3,2},{4,3},{5,4},{6,5},{7,6},{8,7},{9,8},{10,9},{11,1... | collective-permute-start | bytes 786440 | tf_op jit(solution)/shard_map/ppermute | solution.py:19
  141.5 1.9 multiply_reduce_fusion
  146.3 7.5 %collective-permute-done.6 = bf16[128,1024]{0,1:T(8,128)(2,1)} collective-permute-done((bf16[128,1024]{0,1:T(8,128)(2,1)}, bf16[128,1024]{0,1:T(8,128)(2,1)}, u32[]{:S(2)}, u32[]{:S(2)}) %collective-permute-start.6) | collective-permute-done | bytes 262176 | tf_op jit(solution)/shard_map/ppermute | solution.py:19
  157.7 124.6 %all-reduce.1 = (f32[128]{0:T(128)}, f32[128]{0:T(128)}) all-reduce(f32[128]{0:T(128)S(1)} %bitcast_reduce_fusion, f32[128]{0:T(128)S(1)} %bitcast_reduce_fusion.1), channel_id=1, replica_groups=mesh['ctx'=384,'grp'=2] {'ctx','grp'}, use_global_device_ids=true, to_apply=%region_34.35 | all-reduce | flops 256 | bytes 2048 | tf_op jit(solution)/shard_map/psum | solution.py:167
  (256 shorter events, 71.0 us)
Async XLA Ops:
  2.3 21.7 %copy-start.13 = (f32[128,64]{0,1:T(8,128)}, f32[128,64]{0,1:T(8,128)S(1)}, u32[]{:S(2)}) copy-start(f32[128,64]{0,1:T(8,128)S(1)} %get-tuple-element.72) | copy-start | bytes 98308
  2.4 21.7 %copy-start.15 = (f32[128,64]{0,1:T(8,128)}, f32[128,64]{0,1:T(8,128)S(1)}, u32[]{:S(2)}) copy-start(f32[128,64]{0,1:T(8,128)S(1)} %get-tuple-element.73) | copy-start | bytes 98308
  4.9 18.5 %copy-start = (bf16[128,2048]{1,0:T(8,128)(2,1)S(1)}, bf16[128,2048]{1,0:T(8,128)(2,1)}, u32[]{:S(2)}) copy-start(bf16[128,2048]{1,0:T(8,128)(2,1)} %param.8) | copy-start | bytes 1572868
  5.4 18.4 %copy-start.56 = (f32[128]{0:T(128)S(1)}, f32[128]{0:T(128)}, u32[]{:S(2)}) copy-start(f32[128]{0:T(128)} %param.12) | copy-start | bytes 1540
  6.1 38.4 %collective-permute-start = (bf16[128,1024]{1,0:T(8,128)(2,1)}, bf16[128,1024]{1,0:T(8,128)(2,1)}, u32[]{:S(2)}, u32[]{:S(2)}) collective-permute-start(bf16[128,1024]{1,0:T(8,128)(2,1)} %bitcast.531), channel_id=1, source_target_pairs={{0,2},{1,3},{2,4},{3,5},{4,6},{5,7},{6,8},{7,9},{8,10},{9,11},{10,... | collective-permute-start | bytes 786440 | tf_op jit(solution)/shard_map/ppermute | solution.py:19
  10.7 36.5 %collective-permute-start.1 = (bf16[128,1024]{1,0:T(8,128)(2,1)}, bf16[128,1024]{1,0:T(8,128)(2,1)}, u32[]{:S(2)}, u32[]{:S(2)}) collective-permute-start(bf16[128,1024]{1,0:T(8,128)(2,1)} %bitcast.531), channel_id=1, source_target_pairs={{0,1},{1,2},{2,3},{3,4},{4,5},{5,6},{6,7},{7,8},{8,9},{9,10},{10,1... | collective-permute-start | bytes 786440 | tf_op jit(solution)/shard_map/ppermute | solution.py:19
  17.3 28.2 %collective-permute-start.2 = (bf16[128,1024]{1,0:T(8,128)(2,1)}, bf16[128,1024]{1,0:T(8,128)(2,1)}, u32[]{:S(2)}, u32[]{:S(2)}) collective-permute-start(bf16[128,1024]{1,0:T(8,128)(2,1)} %param.10), channel_id=1, source_target_pairs={{0,2},{1,3},{2,4},{3,5},{4,6},{5,7},{6,8},{7,9},{8,10},{9,11},{10,... | collective-permute-start | bytes 786440 | tf_op jit(solution)/shard_map/ppermute | solution.py:19
  19.5 29.6 %collective-permute-start.3 = (bf16[128,1024]{1,0:T(8,128)(2,1)}, bf16[128,1024]{1,0:T(8,128)(2,1)}, u32[]{:S(2)}, u32[]{:S(2)}) collective-permute-start(bf16[128,1024]{1,0:T(8,128)(2,1)} %param.10), channel_id=1, source_target_pairs={{0,1},{1,2},{2,3},{3,4},{4,5},{5,6},{6,7},{7,8},{8,9},{9,10},{10,1... | collective-permute-start | bytes 786440 | tf_op jit(solution)/shard_map/ppermute | solution.py:19
  58.5 7.3 %copy-start.35 = (bf16[128,256]{0,1:T(8,128)(2,1)S(1)}, bf16[128,256]{0,1:T(8,128)(2,1)}, u32[]{:S(2)}) copy-start(bf16[128,256]{0,1:T(8,128)(2,1)} %get-tuple-element.60) | copy-start | bytes 196612
  60.7 7.7 %copy-start.33 = (bf16[128,256]{0,1:T(8,128)(2,1)S(1)}, bf16[128,256]{0,1:T(8,128)(2,1)}, u32[]{:S(2)}) copy-start(bf16[128,256]{0,1:T(8,128)(2,1)} %get-tuple-element.59) | copy-start | bytes 196612
  63.2 7.6 %copy-start.30 = (bf16[128,256]{0,1:T(8,128)(2,1)S(1)}, bf16[128,256]{0,1:T(8,128)(2,1)}, u32[]{:S(2)}) copy-start(bf16[128,256]{0,1:T(8,128)(2,1)} %get-tuple-element.58) | copy-start | bytes 196612
  65.8 7.6 %copy-start.27 = (bf16[128,256]{0,1:T(8,128)(2,1)S(1)}, bf16[128,256]{0,1:T(8,128)(2,1)}, u32[]{:S(2)}) copy-start(bf16[128,256]{0,1:T(8,128)(2,1)} %get-tuple-element.57) | copy-start | bytes 196612
  68.3 7.0 %copy-start.25 = (bf16[128,256]{0,1:T(8,128)(2,1)S(1)}, bf16[128,256]{0,1:T(8,128)(2,1)}, u32[]{:S(2)}) copy-start(bf16[128,256]{0,1:T(8,128)(2,1)} %get-tuple-element.56) | copy-start | bytes 196612
  75.3 12.1 %copy-start.60 = (f32[2,128]{1,0:T(2,128)}, f32[2,128]{1,0:T(2,128)S(1)}, u32[]{:S(2)}) copy-start(f32[2,128]{1,0:T(2,128)S(1)} %get-tuple-element.102) | copy-start | bytes 3076
  77.3 11.7 %copy-start.58 = (f32[2,128]{1,0:T(2,128)}, f32[2,128]{1,0:T(2,128)S(1)}, u32[]{:S(2)}) copy-start(f32[2,128]{1,0:T(2,128)S(1)} %get-tuple-element.106) | copy-start | bytes 3076
  92.9 12.9 %copy-start.26 = (bf16[128,256]{0,1:T(8,128)(2,1)S(1)}, bf16[128,256]{0,1:T(8,128)(2,1)}, u32[]{:S(2)}) copy-start(bf16[128,256]{0,1:T(8,128)(2,1)} %get-tuple-element.56) | copy-start | bytes 196612
  94.9 7.2 %copy-start.31 = (bf16[128,256]{0,1:T(8,128)(2,1)S(1)}, bf16[128,256]{0,1:T(8,128)(2,1)}, u32[]{:S(2)}) copy-start(bf16[128,256]{0,1:T(8,128)(2,1)} %get-tuple-element.58) | copy-start | bytes 196612
  94.9 9.0 %copy-start.28 = (bf16[128,256]{0,1:T(8,128)(2,1)S(1)}, bf16[128,256]{0,1:T(8,128)(2,1)}, u32[]{:S(2)}) copy-start(bf16[128,256]{0,1:T(8,128)(2,1)} %get-tuple-element.57) | copy-start | bytes 196612
  107.6 9.6 %copy-start.39 = (bf16[128,256]{0,1:T(8,128)(2,1)S(1)}, bf16[128,256]{0,1:T(8,128)(2,1)}, u32[]{:S(2)}) copy-start(bf16[128,256]{0,1:T(8,128)(2,1)} %get-tuple-element.62) | copy-start | bytes 196612
  107.6 9.6 %copy-start.68 = (f32[2,128]{1,0:T(2,128)S(1)}, f32[2,128]{1,0:T(2,128)}, u32[]{:S(2)}) copy-start(f32[2,128]{1,0:T(2,128)} %get-tuple-element.82) | copy-start | bytes 3076
  109.1 10.2 %copy-start.38 = (bf16[128,256]{0,1:T(8,128)(2,1)S(1)}, bf16[128,256]{0,1:T(8,128)(2,1)}, u32[]{:S(2)}) copy-start(bf16[128,256]{0,1:T(8,128)(2,1)} %get-tuple-element.61) | copy-start | bytes 196612
  109.9 33.5 %collective-permute-start.5 = (bf16[128,1024]{0,1:T(8,128)(2,1)}, bf16[128,1024]{0,1:T(8,128)(2,1)}, u32[]{:S(2)}, u32[]{:S(2)}) collective-permute-start(bf16[128,1024]{0,1:T(8,128)(2,1)} %get-tuple-element.51), channel_id=1, source_target_pairs={{2,0},{3,1},{4,2},{5,3},{6,4},{7,5},{8,6},{9,7},{10,8},{11,9},{12,... | collective-permute-start | bytes 786440 | tf_op jit(solution)/shard_map/ppermute | solution.py:19
  113.1 8.4 %copy-start.36 = (bf16[128,256]{0,1:T(8,128)(2,1)S(1)}, bf16[128,256]{0,1:T(8,128)(2,1)}, u32[]{:S(2)}) copy-start(bf16[128,256]{0,1:T(8,128)(2,1)} %get-tuple-element.60) | copy-start | bytes 196612
  113.1 8.3 %copy-start.66 = (f32[2,128]{1,0:T(2,128)S(1)}, f32[2,128]{1,0:T(2,128)}, u32[]{:S(2)}) copy-start(f32[2,128]{1,0:T(2,128)} %get-tuple-element.90) | copy-start | bytes 3076
  113.1 30.4 %collective-permute-start.4 = (bf16[128,1024]{0,1:T(8,128)(2,1)}, bf16[128,1024]{0,1:T(8,128)(2,1)}, u32[]{:S(2)}, u32[]{:S(2)}) collective-permute-start(bf16[128,1024]{0,1:T(8,128)(2,1)} %get-tuple-element.50), channel_id=1, source_target_pairs={{1,0},{2,1},{3,2},{4,3},{5,4},{6,5},{7,6},{8,7},{9,8},{10,9},{11,1... | collective-permute-start | bytes 786440 | tf_op jit(solution)/shard_map/ppermute | solution.py:19
  132.1 8.7 %copy-start.43 = (f32[128,16]{1,0:T(8,128)S(1)}, f32[128,16]{1,0:T(8,128)}, u32[]{:S(2)}) copy-start(f32[128,16]{1,0:T(8,128)} %copy.327) | copy-start | bytes 24580
  133.7 7.5 %copy-start.42 = (f32[128,16]{1,0:T(8,128)S(1)}, f32[128,16]{1,0:T(8,128)}, u32[]{:S(2)}) copy-start(f32[128,16]{1,0:T(8,128)} %copy.326) | copy-start | bytes 24580
  134.5 11.8 %collective-permute-start.7 = (bf16[128,1024]{0,1:T(8,128)(2,1)}, bf16[128,1024]{0,1:T(8,128)(2,1)S(1)}, u32[]{:S(2)}, u32[]{:S(2)}) collective-permute-start(bf16[128,1024]{0,1:T(8,128)(2,1)} %get-tuple-element.49), channel_id=1, source_target_pairs={{2,0},{3,1},{4,2},{5,3},{6,4},{7,5},{8,6},{9,7},{10,8},{11,9},{12,... | collective-permute-start | bytes 786440 | tf_op jit(solution)/shard_map/ppermute | solution.py:19
  136.4 17.4 %collective-permute-start.6 = (bf16[128,1024]{0,1:T(8,128)(2,1)}, bf16[128,1024]{0,1:T(8,128)(2,1)}, u32[]{:S(2)}, u32[]{:S(2)}) collective-permute-start(bf16[128,1024]{0,1:T(8,128)(2,1)} %get-tuple-element.48), channel_id=1, source_target_pairs={{1,0},{2,1},{3,2},{4,3},{5,4},{6,5},{7,6},{8,7},{9,8},{10,9},{11,1... | collective-permute-start | bytes 786440 | tf_op jit(solution)/shard_map/ppermute | solution.py:19
  146.1 10.2 %copy-start.41 = (f32[128,8]{1,0:T(8,128)S(1)}, f32[128,8]{1,0:T(8,128)}, u32[]{:S(2)}) copy-start(f32[128,8]{1,0:T(8,128)} %copy.338) | copy-start | bytes 12292
  146.2 10.2 %copy-start.10 = (bf16[128,1024]{1,0:T(8,128)(2,1)S(1)}, bf16[128,1024]{1,0:T(8,128)(2,1)}, u32[]{:S(2)}) copy-start(bf16[128,1024]{1,0:T(8,128)(2,1)} %param.9) | copy-start | bytes 786436
  146.3 10.2 %copy-start.53 = (f32[1024]{0:T(1024)S(1)}, f32[1024]{0:T(1024)}, u32[]{:S(2)}) copy-start(f32[1024]{0:T(1024)} %broadcast_bitcast_fusion.1) | copy-start | bytes 12292
  (45 other events, 104.9 us)
where the time goes:
time: 285 us; the launch traced here: 282 us
  blocking collectives  125 us (44%)
  matrix products  62.3 us (22%)
  local copies, waits for them, and re-layouts  38.3 us (13%)
  starting transfers between devices  30.7 us (11%)
  other arithmetic  17 us (6%)
  waiting for transfers between devices  7.56 us (3%)
    psum x1, blocking collectives, on_device(): lax.psum((query_gain_part, key_gain_part), ('ctx', 'grp'))  125 us
    ppermute x8, starting transfers between devices, from_behind(): lax.ppermute(value, axis, [(source, source + steps) for source in range(i...  30.7 us
    unnamed x155, local copies, waits for them, and re-layouts  22.1 us
    sub x8, matrix products, head_grads(): exps_rows = jnp.exp(scores - row_top)  18.5 us
    dot_general x8, matrix products, head_grads(): jnp.einsum('hqk,qhd->kd', probs_low, grads_out, preferred_element_type=jn...  17.1 us
    dot_general x8, matrix products, head_grads(): jnp.einsum('hqk,qhd->kd', score_grad, queries, preferred_element_type=jnp...  13.6 us
    dot_general x8, matrix products, head_grads(): jnp.einsum('qhd,kd->hqk', grads_out, value_block, preferred_element_type=...  9.73 us
    ppermute x8, waiting for transfers between devices, from_behind(): lax.ppermute(value, axis, [(source, source + steps) for source in range(i...  7.56 us
  transfers between devices with their start and end apart: 8, of which 1 were waited for; matrix products, arithmetic and copies ran while one was open for 17% of the time, Pallas kernels for 0%

commit v1 on v0

v1 whole, which is shorter than its diff:
```python
import functools

import jax
import jax.numpy as jnp
import numpy as np
from jax import lax
from jax.experimental import pallas as pl
from jax.experimental.pallas import tpu as pltpu
from jax.sharding import PartitionSpec as P

HEAD = 128
HALF = HEAD // 2
WINDOW = 256
TOK = 128
KEYS = WINDOW + TOK
EPS = 1e-06
SCALE = 168.0 ** (-0.5)
BASE = 10000.0
MASKED = -1e30
RING = 16
ZS = 12
XS = 4
MESH = pl.DeviceIdType.MESH
F32 = jnp.float32
BF16 = jnp.bfloat16
NT = (((1,), (1,)), ((), ()))
NN = (((1,), (0,)), ((), ()))
TN = (((0,), (0,)), ((), ()))


def place(block):
    return {"ctx": block // 2, "grp": block % 2}


def mm(a, b, dims):
    return lax.dot_general(a, b, dims, preferred_element_type=F32)


def kernel(devices, docs, heads, group, lens_ref, freq_ref, qgain_ref, kgain_ref, q_hbm, k_hbm, v_hbm, g_hbm,
           dq_ref, dk_ref, dv_ref, gains_ref,
           q, go, kv, dkv, term, back, cosd, sins, bias, box, zbox, total,
           load_sem, fs_sem, fr_sem, bs_sem, br_sem, as_sem, ar_sem):
    me = lax.axis_index("ctx") * 2 + lax.axis_index("grp")
    slot_in_ring = me % RING
    ring = me // RING
    z = ring % ZS
    x = ring // ZS
    quad = z % 4
    zgroup = z // 4

    barrier = pltpu.get_barrier_semaphore()

    def greet(block):
        pl.semaphore_signal(barrier, inc=1, device_id=place(block), device_id_type=MESH)

    for hop in (1, 2):
        @pl.when(me >= hop)
        def _():
            greet(me - hop)

        @pl.when(me + hop < devices)
        def _():
            greet(me + hop)

    def ring_peer(i):
        return ring * RING + (slot_in_ring + i) % RING

    def quad_peer(i):
        return (x * ZS + zgroup * 4 + (quad + i) % 4) * RING + slot_in_ring

    def x_peer(i):
        return (((x + i) % XS) * ZS + z) * RING + slot_in_ring

    def group_peer(other):
        return (x * ZS + other * 4 + quad) * RING + slot_in_ring

    @pl.loop(1, RING)
    def _(i):
        greet(ring_peer(i))

    for i in range(1, 4):
        greet(quad_peer(i))
        greet(x_peer(i))

    @pl.when(zgroup == 1)
    def _():
        greet(group_peer(0))
        greet(group_peer(2))

    @pl.when(zgroup != 1)
    def _():
        greet(group_peer(1))

    loads = [
        pltpu.make_async_copy(k_hbm, kv.at[0, 2], load_sem.at[0]),
        pltpu.make_async_copy(v_hbm, kv.at[1, 2], load_sem.at[1]),
        pltpu.make_async_copy(q_hbm, q, load_sem.at[2]),
        pltpu.make_async_copy(g_hbm, go, load_sem.at[3]),
    ]
    for load in loads:
        load.start()

    near = (jnp.minimum(me, 1) + jnp.minimum(me // 2, 1)
            + jnp.minimum(devices - 1 - me, 1) + jnp.minimum((devices - 1 - me) // 2, 1))
    pl.semaphore_wait(barrier, near + (RING - 1) + 3 + 3 + 1 + (zgroup % 2))

    def columns(head):
        return pl.ds(pl.multiple_of(head * HEAD, HEAD), HEAD)

    def forward(hop, which, head):
        source = (k_hbm, v_hbm)[which]
        return pltpu.make_async_remote_copy(
            src_ref=source.at[:, columns(head)],
            dst_ref=kv.at[which, 2 - hop, :, columns(head)],
            send_sem=fs_sem.at[hop - 1, which, head],
            recv_sem=fr_sem.at[hop - 1, which, head],
            device_id=place(lax.rem(me + hop, devices)),
            device_id_type=MESH,
        )

    def backward(hop, which, head):
        return pltpu.make_async_remote_copy(
            src_ref=term.at[which, 2 - hop, :, columns(head)],
            dst_ref=back.at[which, hop - 1, :, columns(head)],
            send_sem=bs_sem.at[hop - 1, which, head],
            recv_sem=br_sem.at[hop - 1, which, head],
            device_id=place(lax.rem(me - hop + devices, devices)),
            device_id_type=MESH,
        )

    @pl.loop(0, heads)
    def _(head):
        for hop in (1, 2):
            @pl.when(me + hop < devices)
            def _():
                for which in (0, 1):
                    forward(hop, which, head).start()

    for hop in (1, 2):
        @pl.when(me < hop)
        def _():
            kv[:, 2 - hop] = jnp.zeros((2, TOK, heads * HEAD), BF16)

        @pl.when(me + hop >= devices)
        def _():
            back[:, hop - 1] = jnp.zeros((2, TOK, heads * HEAD), BF16)

    wide = lens_ref.shape[1]
    lens = lens_ref[...]
    down = lax.broadcasted_iota(jnp.int32, (wide, wide), 0)
    along = lax.broadcasted_iota(jnp.int32, (wide, wide), 1)
    real_down = lax.broadcasted_iota(jnp.int32, (wide, 1), 0) < docs
    real_along = lax.broadcasted_iota(jnp.int32, (1, wide), 1) < docs
    lens_all = jnp.broadcast_to(lens, (wide, wide))
    lens_col = jnp.sum(jnp.where(down == along, lens_all, 0.0), axis=1, keepdims=True)
    ends_row = jnp.sum(jnp.where(down <= along, lens_col, 0.0), axis=0, keepdims=True)
    ends_col = jnp.sum(jnp.where(along <= down, lens_all, 0.0), axis=1, keepdims=True)
    ends_row = jnp.where(real_along, ends_row, 1e9)
    ends_col = jnp.where(real_down, ends_col, 1e9)
    first = (me - 2) * TOK
    key_tok = (first + lax.broadcasted_iota(jnp.int32, (KEYS, 1), 0)).astype(F32)
    own_tok = (first + WINDOW + lax.broadcasted_iota(jnp.int32, (1, TOK), 1)).astype(F32)
    key_before = ends_row <= key_tok
    key_start = jnp.max(jnp.where(key_before, ends_row, 0.0), axis=1, keepdims=True)
    key_doc = jnp.sum(jnp.where(key_before, 1.0, 0.0), axis=1, keepdims=True)
    own_doc = jnp.sum(jnp.where(ends_col <= own_tok, 1.0, 0.0), axis=0, keepdims=True)
    apart = own_tok - key_tok
    visible = (key_doc == own_doc) & (apart >= 0.0) & (apart < float(WINDOW)) & (key_tok >= 0.0)
    bias[...] = jnp.where(visible, 0.0, MASKED)
    angle = (key_tok - key_start) * freq_ref[...]
    cosd[...] = jnp.cos(angle)
    front = lax.broadcasted_iota(jnp.int32, (1, HEAD), 1) < HALF
    sine = jnp.sin(angle)
    sins[...] = jnp.where(front, -sine, sine)

    for load in loads:
        load.wait()

    kgain = kgain_ref[...]
    qgain = qgain_ref[...]
    own = pl.ds(WINDOW, TOK)

    def scale_of(values):
        return lax.rsqrt(jnp.mean(values * values, axis=-1, keepdims=True) + EPS)

    def rotate(normed, cosine, sine):
        return normed * cosine + pltpu.roll(normed, HALF, 1) * sine

    def unrotate(grads, cosine, sine):
        return grads * cosine - pltpu.roll(grads, HALF, 1) * sine

    def raw_grad(grad_normed, values, scale, gain):
        weighted = grad_normed * gain
        return (scale * weighted
                - values * (scale * scale * scale) * jnp.mean(weighted * values, axis=-1, keepdims=True))

    def head_step(head, sums):
        q_sum, k_sum = sums
        for hop in (1, 2):
            @pl.when(me >= hop)
            def _():
                for which in (0, 1):
                    forward(hop, which, head).wait_recv()

        cols = columns(head)
        keys = kv[0, :, :, cols].reshape(KEYS, HEAD).astype(F32)
        values = kv[1, :, :, cols].reshape(KEYS, HEAD)
        k_scale = scale_of(keys)
        k_unit = keys * k_scale
        k_rot = rotate(k_unit * kgain, cosd[...], sins[...]).astype(BF16)
        q_cols = [columns(head * group + i) for i in range(group)]
        q_rot = []
        for c in q_cols:
            raw = q[:, c].astype(F32)
            q_rot.append(rotate(raw * scale_of(raw) * qgain, cosd[own, :], sins[own, :]).astype(BF16))
        q_rot = jnp.concatenate(q_rot, 0)
        g_out = jnp.concatenate([go[:, c] for c in q_cols], 0)
        masks = jnp.concatenate([bias[...]] * group, 1)
        scores = mm(k_rot, q_rot, NT) * SCALE + masks
        top = jnp.max(scores, axis=0, keepdims=True)
        exps = jnp.exp(scores - top)
        probs = exps * (1.0 / jnp.sum(exps, axis=0, keepdims=True))
        prob_grad = mm(values, g_out, NT)
        delta = jnp.sum(probs * prob_grad, axis=0, keepdims=True)
        score_grad = (probs * (prob_grad - delta)).astype(BF16)
        v_term = mm(probs.astype(BF16), g_out, NN)
        k_term = mm(score_grad, q_rot, NN) * SCALE
        v_far = v_term[:WINDOW].astype(BF16)
        k_far = k_term[:WINDOW].astype(BF16)
        term[0, :, :, cols] = k_far.reshape(2, TOK, HEAD)
        term[1, :, :, cols] = v_far.reshape(2, TOK, HEAD)
        for hop in (1, 2):
            @pl.when(me >= hop)
            def _():
                for which in (0, 1):
                    backward(hop, which, head).start()
        dkv[0, :, cols] = k_term[WINDOW:]
        dkv[1, :, cols] = v_term[WINDOW:]
        q_term = mm(score_grad, k_rot, TN) * SCALE
        k_all = jnp.concatenate([k_far.astype(F32), k_term[WINDOW:]], 0)
        k_sum = k_sum + jnp.sum(unrotate(k_all, cosd[...], sins[...]) * k_unit, axis=0, keepdims=True)
        for i, c in enumerate(q_cols):
            raw = q[:, c].astype(F32)
            scale = scale_of(raw)
            normed = unrotate(q_term[i * TOK:(i + 1) * TOK], cosd[own, :], sins[own, :])
            q_sum = q_sum + jnp.sum(normed * raw * scale, axis=0, keepdims=True)
            dq_ref[:, c] = raw_grad(normed, raw, scale, qgain).astype(BF16)
        return q_sum, k_sum

    zero = jnp.zeros((1, HEAD), F32)
    q_sum, k_sum = lax.fori_loop(0, heads, head_step, (zero, zero))

    row = lax.broadcasted_iota(jnp.int32, (8, HEAD), 0)
    part = jnp.where(row == 0, q_sum, jnp.where(row == 1, k_sum, 0.0))

    def message(source, target, index, peer, sem):
        return pltpu.make_async_remote_copy(
            src_ref=source, dst_ref=target, send_sem=as_sem.at[index], recv_sem=ar_sem.at[sem],
            device_id=place(peer), device_id_type=MESH,
        )

    def summed(values):
        out = values[0]
        for value in values[1:]:
            out = out + value
        return out

    def exchange(part, base, count, mine, peer):
        box[base + mine] = part

        @pl.loop(1, count)
        def _(i):
            message(box.at[base + mine], box.at[base + mine], base + i, peer(i), base + mine).start()

        @pl.loop(1, count)
        def _(i):
            there = base + (mine + i) % count
            message(box.at[there], box.at[there], base + i, peer(i), there).wait_recv()

        @pl.loop(1, count)
        def _(i):
            message(box.at[base + mine], box.at[base + mine], base + i, peer(i), base + mine).wait_send()

        return summed([box[base + i] for i in range(count)])

    part = exchange(part, 0, RING, slot_in_ring, ring_peer)
    part = exchange(part, RING, XS, x, x_peer)
    part = exchange(part, RING + XS, 4, quad, quad_peer)
    last = RING + XS + 4
    zbox[zgroup] = part

    def up(g):
        return message(zbox.at[g], zbox.at[g], last + g, group_peer(1), last + g)

    def answer(g):
        return message(total, total, last + g, group_peer(g), last + 1)

    @pl.when(zgroup == 1)
    def _():
        up(0).wait_recv()
        up(2).wait_recv()
        total[...] = zbox[0] + zbox[1] + zbox[2]
        answer(0).start()
        answer(2).start()

    @pl.when(zgroup != 1)
    def _():
        up(zgroup).start()

    @pl.loop(0, heads)
    def _(head):
        for hop in (1, 2):
            @pl.when(me + hop < devices)
            def _():
                for which in (0, 1):
                    backward(hop, which, head).wait_recv()

        cols = columns(head)
        k_grad = dkv[0, :, cols] + back[0, 0, :, cols].astype(F32) + back[0, 1, :, cols].astype(F32)
        v_grad = dkv[1, :, cols] + back[1, 0, :, cols].astype(F32) + back[1, 1, :, cols].astype(F32)
        dv_ref[:, cols] = v_grad.astype(BF16)
        keys = kv[0, 2, :, cols].astype(F32)
        normed = unrotate(k_grad, cosd[own, :], sins[own, :])
        dk_ref[:, cols] = raw_grad(normed, keys, scale_of(keys), kgain).astype(BF16)

    @pl.when(zgroup == 1)
    def _():
        answer(0).wait_send()
        answer(2).wait_send()

    @pl.when(zgroup != 1)
    def _():
        up(zgroup).wait_send()
        answer(1).wait_recv()

    gains_ref[...] = total[...]

    @pl.loop(0, heads)
    def _(head):
        for hop in (1, 2):
            @pl.when(me + hop < devices)
            def _():
                for which in (0, 1):
                    forward(hop, which, head).wait_send()

            @pl.when(me >= hop)
            def _():
                for which in (0, 1):
                    backward(hop, which, head).wait_send()


def on_device(devices, doc_lengths, query_raw, key_raw, value_matrix, out_grad, query_gain, key_gain):
    heads = key_raw.shape[1] // HEAD
    group = query_raw.shape[1] // key_raw.shape[1]
    docs = doc_lengths.shape[0]
    wide = -(-docs // 128) * 128
    lens = jnp.pad(doc_lengths.astype(F32), (0, wide - docs)).reshape(1, wide)
    lane = np.arange(HEAD) % HALF
    freq = jnp.asarray((np.float64(BASE) ** (-2.0 * lane / HEAD)).astype(np.float32).reshape(1, HEAD))
    vmem = pl.BlockSpec(memory_space=pltpu.VMEM)
    anywhere = pl.BlockSpec(memory_space=pl.ANY)
    width = heads * HEAD
    grad_query, grad_key, grad_value, gains = pl.pallas_call(
        functools.partial(kernel, devices, docs, heads, group),
        out_shape=(
            jax.ShapeDtypeStruct(query_raw.shape, BF16),
            jax.ShapeDtypeStruct(key_raw.shape, BF16),
            jax.ShapeDtypeStruct(key_raw.shape, BF16),
            jax.ShapeDtypeStruct((8, HEAD), F32),
        ),
        in_specs=[vmem] * 4 + [anywhere] * 4,
        out_specs=(vmem, vmem, vmem, vmem),
        scratch_shapes=[
            pltpu.VMEM((TOK, width * group), BF16),
            pltpu.VMEM((TOK, width * group), BF16),
            pltpu.VMEM((2, 3, TOK, width), BF16),
            pltpu.VMEM((2, TOK, width), F32),
            pltpu.VMEM((2, 2, TOK, width), BF16),
            pltpu.VMEM((2, 2, TOK, width), BF16),
            pltpu.VMEM((KEYS, HEAD), F32),
            pltpu.VMEM((KEYS, HEAD), F32),
            pltpu.VMEM((KEYS, HEAD), F32),
            pltpu.VMEM((RING + XS + 4, 8, HEAD), F32),
            pltpu.VMEM((3, 8, HEAD), F32),
            pltpu.VMEM((8, HEAD), F32),
            pltpu.SemaphoreType.DMA((4,)),
            pltpu.SemaphoreType.DMA((2, 2, heads)),
            pltpu.SemaphoreType.DMA((2, 2, heads)),
            pltpu.SemaphoreType.DMA((2, 2, heads)),
            pltpu.SemaphoreType.DMA((2, 2, heads)),
            pltpu.SemaphoreType.DMA((RING + XS + 4 + 3,)),
            pltpu.SemaphoreType.DMA((RING + XS + 4 + 3,)),
        ],
        compiler_params=pltpu.CompilerParams(
            collective_id=0, has_side_effects=True, vmem_limit_bytes=56 << 20
        ),
    )(lens, freq, query_gain.reshape(1, HEAD), key_gain.reshape(1, HEAD), query_raw, key_raw, value_matrix, out_grad)
    return grad_query, grad_key, grad_value, gains[0], gains[1]


def solution(mesh):
    devices = mesh.devices.size
    rows = P(("ctx", "grp"), None)
    return jax.shard_map(
        functools.partial(on_device, devices),
        mesh=mesh,
        in_specs=(P(), rows, rows, rows, rows, P(), P()),
        out_specs=(rows, rows, rows, P(), P()),
        check_vma=False,
    )
```

time: 285 us -> 106 us (0.37)
  the two profiles are of different devices: /device:TPU:1 before, /device:TPU:48 now
where the time goes in v1:
time: 106 us
  Pallas kernels  99.3 us (94%)
  local copies, waits for them, and re-layouts  5.51 us (5%)
    pallas_call x1, Pallas kernels, on_device(): pl.pallas_call(functools.partial(kernel, devices, docs, heads, group), ou...  99.3 us
    unnamed x7, local copies, waits for them, and re-layouts  3.67 us

profile of v1, /device:TPU:48, one launch (start us, length us, event | category | flops | bytes accessed | tf_op | source)
XLA Modules:
  0.0 106.1 jit_solution(13394237158657271175)
XLA Ops:
  0.6 0.7 convert_element_type.5
  1.3 0.6 pad.4
  1.9 99.3 %shard_map.119 = (bf16[128,2048]{1,0:T(8,128)(2,1)}, bf16[128,1024]{1,0:T(8,128)(2,1)}, bf16[128,1024]{1,0:T(8,128)(2,1)}, f32[8,128]{1,0:T(8,128)}) custom-call(f32[1,256]{1,0:T(1,128)} %bitcast.7, f32[1,128]{1,0:T(1,128)} %constant.5.clone.freq_ref, f32[1,128]{1,0:T(1,128)} %bitcast.8, f32[1,128]{1,0:T(1,128)} %bitcast.9, bf16[128,2048]{1,0:T(8,128)(2,1)} %q_hbm.1, ...), custom_call_target="tpu_custom_call" | custom-call | tf_op jit(solution)/shard_map/pallas_call | solution.py:363
  101.2 1.3 %slice_bitcast_fusion = (f32[128]{0:T(128)}, f32[128]{0:T(128)}) fusion(f32[8,128]{1,0:T(8,128)} %get-tuple-element.12), kind=kLoop, calls=%fused_computation | loop fusion | bytes 2048 | tf_op jit(solution)/shard_map/squeeze | solution.py:398
  102.4 0.0 copy-start.1
  102.4 1.9 %copy.16 = bf16[128,2048]{1,0:T(8,128)(2,1)} copy(bf16[128,2048]{1,0:T(8,128)(2,1)} %get-tuple-element.20) | data formatting | bytes 1048576
  104.4 0.0 copy-done.1
  104.4 0.0 copy-start
  104.4 0.7 copy.17
  105.1 0.3 copy-done
  105.4 0.7 copy.18
Async XLA Ops:
  102.4 1.9 %copy-start.1 = (bf16[128,1024]{1,0:T(8,128)(2,1)S(1)}, bf16[128,1024]{1,0:T(8,128)(2,1)}, u32[]{:S(2)}) copy-start(bf16[128,1024]{1,0:T(8,128)(2,1)} %get-tuple-element.21) | copy-start | bytes 786436
  104.4 1.0 copy-start

commit v2 on v1

--- a/solution.py
+++ b/solution.py
@@ -17,6 +17,9 @@
 SCALE = 168.0 ** (-0.5)
 BASE = 10000.0
 MASKED = -1e30
+LOG2E = 1.4426950408889634
+AHEAD = 2
+HOLD = 4
 RING = 16
 ZS = 12
 XS = 4
@@ -38,8 +41,8 @@
 
 def kernel(devices, docs, heads, group, lens_ref, freq_ref, qgain_ref, kgain_ref, q_hbm, k_hbm, v_hbm, g_hbm,
            dq_ref, dk_ref, dv_ref, gains_ref,
-           q, go, kv, dkv, term, back, cosd, sins, bias, box, zbox, total,
-           load_sem, fs_sem, fr_sem, bs_sem, br_sem, as_sem, ar_sem):
+           q, go, kv, dkv, term, back, cosd, sins, bias, q_rots, q_scales, k_rots, k_scales, box,
+           load_sem, fs_sem, fr_sem, bs_sem, br_sem, as_sem, ar_sem, ready):
     me = lax.axis_index("ctx") * 2 + lax.axis_index("grp")
     slot_in_ring = me % RING
     ring = me // RING
@@ -74,8 +77,7 @@
     def group_peer(other):
         return (x * ZS + other * 4 + quad) * RING + slot_in_ring
 
-    @pl.loop(1, RING)
-    def _(i):
+    for i in range(1, RING):
         greet(ring_peer(i))
 
     for i in range(1, 4):
@@ -99,10 +101,6 @@
     ]
     for load in loads:
         load.start()
-
-    near = (jnp.minimum(me, 1) + jnp.minimum(me // 2, 1)
-            + jnp.minimum(devices - 1 - me, 1) + jnp.minimum((devices - 1 - me) // 2, 1))
-    pl.semaphore_wait(barrier, near + (RING - 1) + 3 + 3 + 1 + (zgroup % 2))
 
     def columns(head):
         return pl.ds(pl.multiple_of(head * HEAD, HEAD), HEAD)
@@ -128,25 +126,8 @@
             device_id_type=MESH,
         )
 
-    @pl.loop(0, heads)
-    def _(head):
-        for hop in (1, 2):
-            @pl.when(me + hop < devices)
-            def _():
-                for which in (0, 1):
-                    forward(hop, which, head).start()
-
-    for hop in (1, 2):
-        @pl.when(me < hop)
-        def _():
-            kv[:, 2 - hop] = jnp.zeros((2, TOK, heads * HEAD), BF16)
-
-        @pl.when(me + hop >= devices)
-        def _():
-            back[:, hop - 1] = jnp.zeros((2, TOK, heads * HEAD), BF16)
-
-    wide = lens_ref.shape[1]
-    lens = lens_ref[...]
+    wide = -(-docs // 128) * 128
+    lens = jnp.concatenate([lens_ref[...], jnp.zeros((1, wide - docs), jnp.int32)], 1).astype(F32)
     down = lax.broadcasted_iota(jnp.int32, (wide, wide), 0)
     along = lax.broadcasted_iota(jnp.int32, (wide, wide), 1)
     real_down = lax.broadcasted_iota(jnp.int32, (wide, 1), 0) < docs
@@ -167,6 +148,41 @@
     apart = own_tok - key_tok
     visible = (key_doc == own_doc) & (apart >= 0.0) & (apart < float(WINDOW)) & (key_tok >= 0.0)
     bias[...] = jnp.where(visible, 0.0, MASKED)
+    near = (jnp.minimum(me, 1) + jnp.minimum(me // 2, 1)
+            + jnp.minimum(devices - 1 - me, 1) + jnp.minimum((devices - 1 - me) // 2, 1))
+    pl.semaphore_wait(barrier, near + (RING - 1) + 3 + 3 + 1 + (zgroup % 2))
+
+    @pl.when(zgroup == 1)
+    def _():
+        for other in (0, 2):
+            pl.semaphore_signal(ready, inc=1, device_id=place(group_peer(other)), device_id_type=MESH)
+
+    def send_keys(head):
+        for hop in (1, 2):
+            @pl.when(me + hop < devices)
+            def _():
+                for which in (0, 1):
+                    forward(hop, which, head).start()
+
+    def send_terms(head):
+        for hop in (1, 2):
+            @pl.when(me >= hop)
+            def _():
+                for which in (0, 1):
+                    backward(hop, which, head).start()
+
+    for head in range(AHEAD):
+        send_keys(head)
+
+    for hop in (1, 2):
+        @pl.when(me < hop)
+        def _():
+            kv[:, 2 - hop] = jnp.zeros((2, TOK, heads * HEAD), BF16)
+
+        @pl.when(me + hop >= devices)
+        def _():
+            back[:, hop - 1] = jnp.zeros((2, TOK, heads * HEAD), BF16)
+
     angle = (key_tok - key_start) * freq_ref[...]
     cosd[...] = jnp.cos(angle)
     front = lax.broadcasted_iota(jnp.int32, (1, HEAD), 1) < HALF
@@ -180,8 +196,15 @@
     qgain = qgain_ref[...]
     own = pl.ds(WINDOW, TOK)
 
+    share = jnp.full((HEAD, HEAD), 1.0 / HEAD, BF16)
+
+    def mean(values):
+        high = values.astype(BF16)
+        low = (values - high.astype(F32)).astype(BF16)
+        return mm(high, share, NN) + mm(low, share, NN)
+
     def scale_of(values):
-        return lax.rsqrt(jnp.mean(values * values, axis=-1, keepdims=True) + EPS)
+        return lax.rsqrt(mean(values * values) + EPS)
 
     def rotate(normed, cosine, sine):
         return normed * cosine + pltpu.roll(normed, HALF, 1) * sine
@@ -189,62 +212,81 @@
     def unrotate(grads, cosine, sine):
         return grads * cosine - pltpu.roll(grads, HALF, 1) * sine
 
-    def raw_grad(grad_normed, values, scale, gain):
+    def raw_grad(grad_normed, unit, scale, gain):
         weighted = grad_normed * gain
-        return (scale * weighted
-                - values * (scale * scale * scale) * jnp.mean(weighted * values, axis=-1, keepdims=True))
+        return scale * (weighted - unit * mean(weighted * unit))
+
+    @pl.loop(0, heads)
+    def _(head):
+        cosine, sine = cosd[own, :], sins[own, :]
+        raw = kv[0, 2, :, columns(head)].astype(F32)
+        scale = scale_of(raw)
+        k_scales[head] = scale
+        k_rots[head] = rotate(raw * scale * kgain, cosine, sine).astype(BF16)
+        for i in range(group):
+            raw = q[:, columns(head * group + i)].astype(F32)
+            scale = scale_of(raw)
+            q_scales[head, pl.ds(i * TOK, TOK), :] = scale
+            q_rots[head, pl.ds(i * TOK, TOK), :] = rotate(raw * scale * qgain, cosine, sine).astype(BF16)
 
     def head_step(head, sums):
         q_sum, k_sum = sums
         for hop in (1, 2):
+            @pl.when((me + hop < devices) & (head + AHEAD < heads))
+            def _():
+                for which in (0, 1):
+                    forward(hop, which, head).wait_send()
+                for which in (0, 1):
+                    forward(hop, which, head + AHEAD).start()
+
+        for hop in (1, 2):
             @pl.when(me >= hop)
             def _():
                 for which in (0, 1):
                     forward(hop, which, head).wait_recv()
 
         cols = columns(head)
-        keys = kv[0, :, :, cols].reshape(KEYS, HEAD).astype(F32)
+        keys = kv[0, :2, :, cols].reshape(WINDOW, HEAD).astype(F32)
         values = kv[1, :, :, cols].reshape(KEYS, HEAD)
-        k_scale = scale_of(keys)
-        k_unit = keys * k_scale
-        k_rot = rotate(k_unit * kgain, cosd[...], sins[...]).astype(BF16)
+        k_unit = keys * scale_of(keys)
+        past = pl.ds(0, WINDOW)
+        k_rot = jnp.concatenate([rotate(k_unit * kgain, cosd[past, :], sins[past, :]).astype(BF16), k_rots[head]], 0)
+        k_unit = jnp.concatenate([k_unit, kv[0, 2, :, cols].astype(F32) * k_scales[head]], 0)
         q_cols = [columns(head * group + i) for i in range(group)]
-        q_rot = []
-        for c in q_cols:
-            raw = q[:, c].astype(F32)
-            q_rot.append(rotate(raw * scale_of(raw) * qgain, cosd[own, :], sins[own, :]).astype(BF16))
-        q_rot = jnp.concatenate(q_rot, 0)
+        q_rot = q_rots[head]
         g_out = jnp.concatenate([go[:, c] for c in q_cols], 0)
         masks = jnp.concatenate([bias[...]] * group, 1)
-        scores = mm(k_rot, q_rot, NT) * SCALE + masks
+        scores = mm(k_rot, q_rot, NT) + masks
+        prob_grad = mm(values, g_out, NT)
         top = jnp.max(scores, axis=0, keepdims=True)
-        exps = jnp.exp(scores - top)
+        exps = jnp.exp2((scores - top) * (SCALE * LOG2E))
         probs = exps * (1.0 / jnp.sum(exps, axis=0, keepdims=True))
-        prob_grad = mm(values, g_out, NT)
         delta = jnp.sum(probs * prob_grad, axis=0, keepdims=True)
         score_grad = (probs * (prob_grad - delta)).astype(BF16)
         v_term = mm(probs.astype(BF16), g_out, NN)
         k_term = mm(score_grad, q_rot, NN) * SCALE
+        q_term = mm(score_grad, k_rot, TN) * SCALE
         v_far = v_term[:WINDOW].astype(BF16)
         k_far = k_term[:WINDOW].astype(BF16)
         term[0, :, :, cols] = k_far.reshape(2, TOK, HEAD)
         term[1, :, :, cols] = v_far.reshape(2, TOK, HEAD)
-        for hop in (1, 2):
-            @pl.when(me >= hop)
-            def _():
-                for which in (0, 1):
-                    backward(hop, which, head).start()
         dkv[0, :, cols] = k_term[WINDOW:]
         dkv[1, :, cols] = v_term[WINDOW:]
-        q_term = mm(score_grad, k_rot, TN) * SCALE
         k_all = jnp.concatenate([k_far.astype(F32), k_term[WINDOW:]], 0)
         k_sum = k_sum + jnp.sum(unrotate(k_all, cosd[...], sins[...]) * k_unit, axis=0, keepdims=True)
         for i, c in enumerate(q_cols):
-            raw = q[:, c].astype(F32)
-            scale = scale_of(raw)
+            scale = q_scales[head, pl.ds(i * TOK, TOK), :]
+            unit = q[:, c].astype(F32) * scale
             normed = unrotate(q_term[i * TOK:(i + 1) * TOK], cosd[own, :], sins[own, :])
-            q_sum = q_sum + jnp.sum(normed * raw * scale, axis=0, keepdims=True)
-            dq_ref[:, c] = raw_grad(normed, raw, scale, qgain).astype(BF16)
+            q_sum = q_sum + jnp.sum(normed * unit, axis=0, keepdims=True)
+            dq_ref[:, c] = raw_grad(normed, unit, scale, qgain).astype(BF16)
+
+        for hop in (1, 2):
+            @pl.when((me >= hop) & (head >= HOLD))
+            def _():
+                for which in (0, 1):
+                    backward(hop, which, head - HOLD).start()
+
         return q_sum, k_sum
 
     zero = jnp.zeros((1, HEAD), F32)
@@ -265,47 +307,45 @@
             out = out + value
         return out
 
-    def exchange(part, base, count, mine, peer):
+    pending = []
+
+    def launch(part, base, count, mine, peer):
         box[base + mine] = part
-
-        @pl.loop(1, count)
-        def _(i):
-            message(box.at[base + mine], box.at[base + mine], base + i, peer(i), base + mine).start()
-
-        @pl.loop(1, count)
-        def _(i):
+        for i in range(1, count):
+            copy = message(box.at[base + mine], box.at[base + mine], base + i, peer(i), base + mine)
+            copy.start()
+            pending.append(copy)
+
+    def collect(base, count, mine, peer):
+        for i in range(1, count):
             there = base + (mine + i) % count
             message(box.at[there], box.at[there], base + i, peer(i), there).wait_recv()
-
-        @pl.loop(1, count)
-        def _(i):
-            message(box.at[base + mine], box.at[base + mine], base + i, peer(i), base + mine).wait_send()
-
         return summed([box[base + i] for i in range(count)])
 
-    part = exchange(part, 0, RING, slot_in_ring, ring_peer)
-    part = exchange(part, RING, XS, x, x_peer)
-    part = exchange(part, RING + XS, 4, quad, quad_peer)
+    launch(part, 0, RING, slot_in_ring, ring_peer)
+    for head in range(heads - HOLD, heads - HOLD + 1):
+        send_terms(head)
+    part = collect(0, RING, slot_in_ring, ring_peer)
+    launch(part, RING, XS, x, x_peer)
+    for head in range(heads - HOLD + 1, heads - HOLD + 2):
+        send_terms(head)
+    part = collect(RING, XS, x, x_peer)
+    launch(part, RING + XS, 4, quad, quad_peer)
+    for head in range(heads - HOLD + 2, heads - HOLD + 3):
+        send_terms(head)
+    part = collect(RING + XS, 4, quad, quad_peer)
     last = RING + XS + 4
-    zbox[zgroup] = part
-
-    def up(g):
-        return message(zbox.at[g], zbox.at[g], last + g, group_peer(1), last + g)
-
-    def answer(g):
-        return message(total, total, last + g, group_peer(g), last + 1)
-
-    @pl.when(zgroup == 1)
-    def _():
-        up(0).wait_recv()
-        up(2).wait_recv()
-        total[...] = zbox[0] + zbox[1] + zbox[2]
-        answer(0).start()
-        answer(2).start()
+
+    def far_peer(i):
+        return group_peer((zgroup + i) % 3)
 
     @pl.when(zgroup != 1)
     def _():
-        up(zgroup).start()
+        pl.semaphore_wait(ready, 1)
+
+    launch(part, last, 3, zgroup, far_peer)
+    for head in range(heads - HOLD + 3, heads):
+        send_terms(head)
 
     @pl.loop(0, heads)
     def _(head):
@@ -319,42 +359,48 @@
         k_grad = dkv[0, :, cols] + back[0, 0, :, cols].astype(F32) + back[0, 1, :, cols].astype(F32)
         v_grad = dkv[1, :, cols] + back[1, 0, :, cols].astype(F32) + back[1, 1, :, cols].astype(F32)
         dv_ref[:, cols] = v_grad.astype(BF16)
-        keys = kv[0, 2, :, cols].astype(F32)
+        scale = k_scales[head]
+        unit = kv[0, 2, :, cols].astype(F32) * scale
         normed = unrotate(k_grad, cosd[own, :], sins[own, :])
-        dk_ref[:, cols] = raw_grad(normed, keys, scale_of(keys), kgain).astype(BF16)
-
-    @pl.when(zgroup == 1)
-    def _():
-        answer(0).wait_send()
-        answer(2).wait_send()
-
-    @pl.when(zgroup != 1)
-    def _():
-        up(zgroup).wait_send()
-        answer(1).wait_recv()
-
-    gains_ref[...] = total[...]
-
-    @pl.loop(0, heads)
-    def _(head):
-        for hop in (1, 2):
-            @pl.when(me + hop < devices)
-            def _():
+        dk_ref[:, cols] = raw_grad(normed, unit, scale, kgain).astype(BF16)
+
+    gains_ref[...] = collect(last, 3, zgroup, far_peer)
+    for copy in pending:
+        copy.wait_send()
+
+    for hop in (1, 2):
+        @pl.when(me + hop < devices)
+        def _():
+            for head in range(heads - AHEAD, heads):
                 for which in (0, 1):
                     forward(hop, which, head).wait_send()
 
-            @pl.when(me >= hop)
-            def _():
+        @pl.when(me >= hop)
+        def _():
+            for head in range(heads):
                 for which in (0, 1):
                     backward(hop, which, head).wait_send()
+
+
+def finish(dq_in, dk_in, dv_in, gains_in, dq, dk, dv, q_gain, k_gain, sems):
+    copies = [
+        pltpu.make_async_copy(dq_in, dq, sems.at[0]),
+        pltpu.make_async_copy(dk_in, dk, sems.at[1]),
+        pltpu.make_async_copy(dv_in, dv, sems.at[2]),
+    ]
+    for copy in copies:
+        copy.start()
+    q_gain[...] = gains_in[0:1, :]
+    k_gain[...] = gains_in[1:2, :]
+    for copy in copies:
+        copy.wait()
 
 
 def on_device(devices, doc_lengths, query_raw, key_raw, value_matrix, out_grad, query_gain, key_gain):
     heads = key_raw.shape[1] // HEAD
     group = query_raw.shape[1] // key_raw.shape[1]
     docs = doc_lengths.shape[0]
-    wide = -(-docs // 128) * 128
-    lens = jnp.pad(doc_lengths.astype(F32), (0, wide - docs)).reshape(1, wide)
+    lens = doc_lengths.reshape(1, docs)
     lane = np.arange(HEAD) % HALF
     freq = jnp.asarray((np.float64(BASE) ** (-2.0 * lane / HEAD)).astype(np.float32).reshape(1, HEAD))
     vmem = pl.BlockSpec(memory_space=pltpu.VMEM)
@@ -380,9 +426,11 @@
             pltpu.VMEM((KEYS, HEAD), F32),
             pltpu.VMEM((KEYS, HEAD), F32),
             pltpu.VMEM((KEYS, HEAD), F32),
-            pltpu.VMEM((RING + XS + 4, 8, HEAD), F32),
-            pltpu.VMEM((3, 8, HEAD), F32),
-            pltpu.VMEM((8, HEAD), F32),
+            pltpu.VMEM((heads, group * TOK, HEAD), BF16),
+            pltpu.VMEM((heads, group * TOK, HEAD), F32),
+            pltpu.VMEM((heads, TOK, HEAD), BF16),
+            pltpu.VMEM((heads, TOK, HEAD), F32),
+            pltpu.VMEM((RING + XS + 4 + 3, 8, HEAD), F32),
             pltpu.SemaphoreType.DMA((4,)),
             pltpu.SemaphoreType.DMA((2, 2, heads)),
             pltpu.SemaphoreType.DMA((2, 2, heads)),
@@ -390,12 +438,26 @@
             pltpu.SemaphoreType.DMA((2, 2, heads)),
             pltpu.SemaphoreType.DMA((RING + XS + 4 + 3,)),
             pltpu.SemaphoreType.DMA((RING + XS + 4 + 3,)),
+            pltpu.SemaphoreType.REGULAR,
         ],
         compiler_params=pltpu.CompilerParams(
             collective_id=0, has_side_effects=True, vmem_limit_bytes=56 << 20
         ),
     )(lens, freq, query_gain.reshape(1, HEAD), key_gain.reshape(1, HEAD), query_raw, key_raw, value_matrix, out_grad)
-    return grad_query, grad_key, grad_value, gains[0], gains[1]
+    grad_query, grad_key, grad_value, q_gain, k_gain = pl.pallas_call(
+        finish,
+        out_shape=(
+            jax.ShapeDtypeStruct(query_raw.shape, BF16),
+            jax.ShapeDtypeStruct(key_raw.shape, BF16),
+            jax.ShapeDtypeStruct(key_raw.shape, BF16),
+            jax.ShapeDtypeStruct((1, HEAD), F32),
+            jax.ShapeDtypeStruct((1, HEAD), F32),
+        ),
+        in_specs=[vmem] * 4,
+        out_specs=(anywhere, anywhere, anywhere, vmem, vmem),
+        scratch_shapes=[pltpu.SemaphoreType.DMA((3,))],
+    )(grad_query, grad_key, grad_value, gains)
+    return grad_query, grad_key, grad_value, q_gain.reshape(HEAD), k_gain.reshape(HEAD)
 
 
 def solution(mesh):

time: 106 us -> 91.5 us (0.86)
  the two profiles are of different devices: /device:TPU:48 before, /device:TPU:1 now
where the time goes in v2:
time: 91.5 us; the launch traced here: 91.3 us
  Pallas kernels  90.6 us (99%)
    pallas_call x1, Pallas kernels, on_device(): pl.pallas_call(functools.partial(kernel, devices, docs, heads, group), ou...  87.9 us
    pallas_call x1, Pallas kernels, on_device(): pl.pallas_call(finish, out_shape=(jax.ShapeDtypeStruct(query_raw.shape, B...  2.69 us

profile of v2, /device:TPU:1, one launch (start us, length us, event | category | flops | bytes accessed | tf_op | source)
XLA Modules:
  0.0 91.3 jit_solution(11447247988529781681)
XLA Ops:
  0.6 87.9 %shard_map.119 = (bf16[128,2048]{1,0:T(8,128)(2,1)}, bf16[128,1024]{1,0:T(8,128)(2,1)}, bf16[128,1024]{1,0:T(8,128)(2,1)}, f32[8,128]{1,0:T(8,128)}) custom-call(s32[1,192]{1,0:T(1,128)} %bitcast.5, f32[1,128]{1,0:T(1,128)} %constant.2.clone.freq_ref, f32[1,128]{1,0:T(1,128)} %bitcast.6, f32[1,128]{1,0:T(1,128)} %bitcast.7, bf16[128,2048]{1,0:T(8,128)(2,1)} %q_hbm.1, ...), custom_call_target="tpu_custom_call" | custom-call | tf_op jit(solution)/shard_map/pallas_call | solution.py:409
  88.6 2.7 %shard_map.120 = (bf16[128,2048]{1,0:T(8,128)(2,1)}, bf16[128,1024]{1,0:T(8,128)(2,1)}, bf16[128,1024]{1,0:T(8,128)(2,1)}, f32[1,128]{1,0:T(1,128)}, f32[1,128]{1,0:T(1,128)}) custom-call(bf16[128,2048]{1,0:T(8,128)(2,1)} %get-tuple-element.14.dq_in, bf16[128,1024]{1,0:T(8,128)(2,1)} %get-tuple-element.15.dk_in, bf16[128,1024]{1,0:T(8,128)(2,1)} %get-tuple-element.16.dv_in, ...), custom_call_target="tpu_custom_call" | custom-call | tf_op jit(solution)/shard_map/pallas_call | solution.py:447

commit v3 on v2

--- a/solution.py
+++ b/solution.py
@@ -18,7 +18,6 @@
 BASE = 10000.0
 MASKED = -1e30
 LOG2E = 1.4426950408889634
-AHEAD = 2
 HOLD = 4
 RING = 16
 ZS = 12
@@ -40,9 +39,9 @@
 
 
 def kernel(devices, docs, heads, group, lens_ref, freq_ref, qgain_ref, kgain_ref, q_hbm, k_hbm, v_hbm, g_hbm,
-           dq_ref, dk_ref, dv_ref, gains_ref,
-           q, go, kv, dkv, term, back, cosd, sins, bias, q_rots, q_scales, k_rots, k_scales, box,
-           load_sem, fs_sem, fr_sem, bs_sem, br_sem, as_sem, ar_sem, ready):
+           dq_hbm, dk_hbm, dv_hbm, gains_ref,
+           dq_ref, dk_ref, dv_ref, q, go, kv, dkv, term, back, cosd, sins, bias, q_rots, q_scales, k_rots, k_scales, box,
+           load_sem, fs_sem, fr_sem, bs_sem, br_sem, as_sem, ar_sem, out_sem, ready):
     me = lax.axis_index("ctx") * 2 + lax.axis_index("grp")
     slot_in_ring = me % RING
     ring = me // RING
@@ -125,6 +124,42 @@
             device_id=place(lax.rem(me - hop + devices, devices)),
             device_id_type=MESH,
         )
+
+    near = (jnp.minimum(me, 1) + jnp.minimum(me // 2, 1)
+            + jnp.minimum(devices - 1 - me, 1) + jnp.minimum((devices - 1 - me) // 2, 1))
+    pl.semaphore_wait(barrier, near + (RING - 1) + 3 + 3 + 1 + (zgroup % 2))
+
+    @pl.when(zgroup == 1)
+    def _():
+        for other in (0, 2):
+            pl.semaphore_signal(ready, inc=1, device_id=place(group_peer(other)), device_id_type=MESH)
+
+    def send_keys(head):
+        for hop in (1, 2):
+            @pl.when(me + hop < devices)
+            def _():
+                for which in (0, 1):
+                    forward(hop, which, head).start()
+
+    def send_terms(head):
+        for hop in (1, 2):
+            @pl.when(me >= hop)
+            def _():
+                for which in (0, 1):
+                    backward(hop, which, head).start()
+
+    @pl.loop(0, heads)
+    def _(head):
+        send_keys(head)
+
+    for hop in (1, 2):
+        @pl.when(me < hop)
+        def _():
+            kv[:, 2 - hop] = jnp.zeros((2, TOK, heads * HEAD), BF16)
+
+        @pl.when(me + hop >= devices)
+        def _():
+            back[:, hop - 1] = jnp.zeros((2, TOK, heads * HEAD), BF16)
 
     wide = -(-docs // 128) * 128
     lens = jnp.concatenate([lens_ref[...], jnp.zeros((1, wide - docs), jnp.int32)], 1).astype(F32)
@@ -148,41 +183,6 @@
     apart = own_tok - key_tok
     visible = (key_doc == own_doc) & (apart >= 0.0) & (apart < float(WINDOW)) & (key_tok >= 0.0)
     bias[...] = jnp.where(visible, 0.0, MASKED)
-    near = (jnp.minimum(me, 1) + jnp.minimum(me // 2, 1)
-            + jnp.minimum(devices - 1 - me, 1) + jnp.minimum((devices - 1 - me) // 2, 1))
-    pl.semaphore_wait(barrier, near + (RING - 1) + 3 + 3 + 1 + (zgroup % 2))
-
-    @pl.when(zgroup == 1)
-    def _():
-        for other in (0, 2):
-            pl.semaphore_signal(ready, inc=1, device_id=place(group_peer(other)), device_id_type=MESH)
-
-    def send_keys(head):
-        for hop in (1, 2):
-            @pl.when(me + hop < devices)
-            def _():
-                for which in (0, 1):
-                    forward(hop, which, head).start()
-
-    def send_terms(head):
-        for hop in (1, 2):
-            @pl.when(me >= hop)
-            def _():
-                for which in (0, 1):
-                    backward(hop, which, head).start()
-
-    for head in range(AHEAD):
-        send_keys(head)
-
-    for hop in (1, 2):
-        @pl.when(me < hop)
-        def _():
-            kv[:, 2 - hop] = jnp.zeros((2, TOK, heads * HEAD), BF16)
-
-        @pl.when(me + hop >= devices)
-        def _():
-            back[:, hop - 1] = jnp.zeros((2, TOK, heads * HEAD), BF16)
-
     angle = (key_tok - key_start) * freq_ref[...]
     cosd[...] = jnp.cos(angle)
     front = lax.broadcasted_iota(jnp.int32, (1, HEAD), 1) < HALF
@@ -229,16 +229,10 @@
             q_scales[head, pl.ds(i * TOK, TOK), :] = scale
             q_rots[head, pl.ds(i * TOK, TOK), :] = rotate(raw * scale * qgain, cosine, sine).astype(BF16)
 
+    hold = HOLD
+
     def head_step(head, sums):
         q_sum, k_sum = sums
-        for hop in (1, 2):
-            @pl.when((me + hop < devices) & (head + AHEAD < heads))
-            def _():
-                for which in (0, 1):
-                    forward(hop, which, head).wait_send()
-                for which in (0, 1):
-                    forward(hop, which, head + AHEAD).start()
-
         for hop in (1, 2):
             @pl.when(me >= hop)
             def _():
@@ -282,18 +276,17 @@
             dq_ref[:, c] = raw_grad(normed, unit, scale, qgain).astype(BF16)
 
         for hop in (1, 2):
-            @pl.when((me >= hop) & (head >= HOLD))
+            @pl.when((me >= hop) & (head >= hold))
             def _():
                 for which in (0, 1):
-                    backward(hop, which, head - HOLD).start()
+                    backward(hop, which, head - hold).start()
 
         return q_sum, k_sum
 
     zero = jnp.zeros((1, HEAD), F32)
     q_sum, k_sum = lax.fori_loop(0, heads, head_step, (zero, zero))
 
-    row = lax.broadcasted_iota(jnp.int32, (8, HEAD), 0)
-    part = jnp.where(row == 0, q_sum, jnp.where(row == 1, k_sum, 0.0))
+    part = jnp.concatenate([q_sum, k_sum], 0)
 
     def message(source, target, index, peer, sem):
         return pltpu.make_async_remote_copy(
@@ -322,17 +315,16 @@
             message(box.at[there], box.at[there], base + i, peer(i), there).wait_recv()
         return summed([box[base + i] for i in range(count)])
 
+    dq_copy = pltpu.make_async_copy(dq_ref, dq_hbm, out_sem.at[0])
     launch(part, 0, RING, slot_in_ring, ring_peer)
-    for head in range(heads - HOLD, heads - HOLD + 1):
-        send_terms(head)
+    dq_copy.start()
+    send_terms(heads - hold)
     part = collect(0, RING, slot_in_ring, ring_peer)
     launch(part, RING, XS, x, x_peer)
-    for head in range(heads - HOLD + 1, heads - HOLD + 2):
-        send_terms(head)
+    send_terms(heads - hold + 1)
     part = collect(RING, XS, x, x_peer)
     launch(part, RING + XS, 4, quad, quad_peer)
-    for head in range(heads - HOLD + 2, heads - HOLD + 3):
-        send_terms(head)
+    send_terms(heads - hold + 2)
     part = collect(RING + XS, 4, quad, quad_peer)
     last = RING + XS + 4
 
@@ -344,7 +336,9 @@
         pl.semaphore_wait(ready, 1)
 
     launch(part, last, 3, zgroup, far_peer)
-    for head in range(heads - HOLD + 3, heads):
+
+    @pl.loop(heads - hold + 3, heads)
+    def _(head):
         send_terms(head)
 
     @pl.loop(0, heads)
@@ -364,14 +358,20 @@
         normed = unrotate(k_grad, cosd[own, :], sins[own, :])
         dk_ref[:, cols] = raw_grad(normed, unit, scale, kgain).astype(BF16)
 
+    outs = [pltpu.make_async_copy(dk_ref, dk_hbm, out_sem.at[1]), pltpu.make_async_copy(dv_ref, dv_hbm, out_sem.at[2])]
+    for out in outs:
+        out.start()
     gains_ref[...] = collect(last, 3, zgroup, far_peer)
     for copy in pending:
         copy.wait_send()
+    dq_copy.wait()
+    for out in outs:
+        out.wait()
 
     for hop in (1, 2):
         @pl.when(me + hop < devices)
         def _():
-            for head in range(heads - AHEAD, heads):
+            for head in range(heads):
                 for which in (0, 1):
                     forward(hop, which, head).wait_send()
 
@@ -412,11 +412,14 @@
             jax.ShapeDtypeStruct(query_raw.shape, BF16),
             jax.ShapeDtypeStruct(key_raw.shape, BF16),
             jax.ShapeDtypeStruct(key_raw.shape, BF16),
-            jax.ShapeDtypeStruct((8, HEAD), F32),
+            jax.ShapeDtypeStruct((2, HEAD), F32),
         ),
         in_specs=[vmem] * 4 + [anywhere] * 4,
-        out_specs=(vmem, vmem, vmem, vmem),
+        out_specs=(anywhere, anywhere, anywhere, vmem),
         scratch_shapes=[
+            pltpu.VMEM((TOK, width * group), BF16),
+            pltpu.VMEM((TOK, width), BF16),
+            pltpu.VMEM((TOK, width), BF16),
             pltpu.VMEM((TOK, width * group), BF16),
             pltpu.VMEM((TOK, width * group), BF16),
             pltpu.VMEM((2, 3, TOK, width), BF16),
@@ -430,7 +433,7 @@
             pltpu.VMEM((heads, group * TOK, HEAD), F32),
             pltpu.VMEM((heads, TOK, HEAD), BF16),
             pltpu.VMEM((heads, TOK, HEAD), F32),
-            pltpu.VMEM((RING + XS + 4 + 3, 8, HEAD), F32),
+            pltpu.VMEM((RING + XS + 4 + 3, 2, HEAD), F32),
             pltpu.SemaphoreType.DMA((4,)),
             pltpu.SemaphoreType.DMA((2, 2, heads)),
             pltpu.SemaphoreType.DMA((2, 2, heads)),
@@ -438,6 +441,7 @@
             pltpu.SemaphoreType.DMA((2, 2, heads)),
             pltpu.SemaphoreType.DMA((RING + XS + 4 + 3,)),
             pltpu.SemaphoreType.DMA((RING + XS + 4 + 3,)),
+            pltpu.SemaphoreType.DMA((3,)),
             pltpu.SemaphoreType.REGULAR,
         ],
         compiler_params=pltpu.CompilerParams(

time: 91.5 us -> 89.2 us (0.975)
  the two profiles are of different devices: /device:TPU:1 before, /device:TPU:7 now
where the time goes in v3:
time: 89.2 us; the launch traced here: 89 us
  Pallas kernels  88.4 us (99%)
    pallas_call x1, Pallas kernels, on_device(): pl.pallas_call(functools.partial(kernel, devices, docs, heads, group), ou...  85.7 us
    pallas_call x1, Pallas kernels, on_device(): pl.pallas_call(finish, out_shape=(jax.ShapeDtypeStruct(query_raw.shape, B...  2.69 us

profile of v3, /device:TPU:7, one launch (start us, length us, event | category | flops | bytes accessed | tf_op | source)
XLA Modules:
  0.0 89.0 jit_solution(5950016932631647591)
XLA Ops:
  0.6 85.7 %shard_map.119 = (bf16[128,2048]{1,0:T(8,128)(2,1)}, bf16[128,1024]{1,0:T(8,128)(2,1)}, bf16[128,1024]{1,0:T(8,128)(2,1)}, f32[2,128]{1,0:T(2,128)}) custom-call(s32[1,192]{1,0:T(1,128)} %bitcast.5, f32[1,128]{1,0:T(1,128)} %constant.2.clone.freq_ref, f32[1,128]{1,0:T(1,128)} %bitcast.6, f32[1,128]{1,0:T(1,128)} %bitcast.7, bf16[128,2048]{1,0:T(8,128)(2,1)} %q_hbm.1, ...), custom_call_target="tpu_custom_call" | custom-call | tf_op jit(solution)/shard_map/pallas_call | solution.py:409
  86.3 2.7 %shard_map.120 = (bf16[128,2048]{1,0:T(8,128)(2,1)}, bf16[128,1024]{1,0:T(8,128)(2,1)}, bf16[128,1024]{1,0:T(8,128)(2,1)}, f32[1,128]{1,0:T(1,128)}, f32[1,128]{1,0:T(1,128)}) custom-call(bf16[128,2048]{1,0:T(8,128)(2,1)} %get-tuple-element.14.dq_in, bf16[128,1024]{1,0:T(8,128)(2,1)} %get-tuple-element.15.dk_in, bf16[128,1024]{1,0:T(8,128)(2,1)} %get-tuple-element.16.dv_in, ...), custom_call_target="tpu_custom_call" | custom-call | tf_op jit(solution)/shard_map/pallas_call | solution.py:451

commit v4 on v3

--- a/solution.py
+++ b/solution.py
@@ -21,7 +21,7 @@
 HOLD = 4
 RING = 16
 ZS = 12
-XS = 4
+NEAR = 16
 MESH = pl.DeviceIdType.MESH
 F32 = jnp.float32
 BF16 = jnp.bfloat16
@@ -67,11 +67,11 @@
     def ring_peer(i):
         return ring * RING + (slot_in_ring + i) % RING
 
-    def quad_peer(i):
-        return (x * ZS + zgroup * 4 + (quad + i) % 4) * RING + slot_in_ring
-
-    def x_peer(i):
-        return (((x + i) % XS) * ZS + z) * RING + slot_in_ring
+    near_slot = x * 4 + quad
+
+    def near_peer(i):
+        there = (near_slot + i) % NEAR
+        return ((there // 4) * ZS + zgroup * 4 + there % 4) * RING + slot_in_ring
 
     def group_peer(other):
         return (x * ZS + other * 4 + quad) * RING + slot_in_ring
@@ -79,9 +79,8 @@
     for i in range(1, RING):
         greet(ring_peer(i))
 
-    for i in range(1, 4):
-        greet(quad_peer(i))
-        greet(x_peer(i))
+    for i in range(1, NEAR):
+        greet(near_peer(i))
 
     @pl.when(zgroup == 1)
     def _():
@@ -127,7 +126,7 @@
 
     near = (jnp.minimum(me, 1) + jnp.minimum(me // 2, 1)
             + jnp.minimum(devices - 1 - me, 1) + jnp.minimum((devices - 1 - me) // 2, 1))
-    pl.semaphore_wait(barrier, near + (RING - 1) + 3 + 3 + 1 + (zgroup % 2))
+    pl.semaphore_wait(barrier, near + (RING - 1) + (NEAR - 1) + 1 + (zgroup % 2))
 
     @pl.when(zgroup == 1)
     def _():
@@ -319,14 +318,12 @@
     launch(part, 0, RING, slot_in_ring, ring_peer)
     dq_copy.start()
     send_terms(heads - hold)
+    send_terms(heads - hold + 1)
     part = collect(0, RING, slot_in_ring, ring_peer)
-    launch(part, RING, XS, x, x_peer)
-    send_terms(heads - hold + 1)
-    part = collect(RING, XS, x, x_peer)
-    launch(part, RING + XS, 4, quad, quad_peer)
+    launch(part, RING, NEAR, near_slot, near_peer)
     send_terms(heads - hold + 2)
-    part = collect(RING + XS, 4, quad, quad_peer)
-    last = RING + XS + 4
+    part = collect(RING, NEAR, near_slot, near_peer)
+    last = RING + NEAR
 
     def far_peer(i):
         return group_peer((zgroup + i) % 3)
@@ -433,14 +430,14 @@
             pltpu.VMEM((heads, group * TOK, HEAD), F32),
             pltpu.VMEM((heads, TOK, HEAD), BF16),
             pltpu.VMEM((heads, TOK, HEAD), F32),
-            pltpu.VMEM((RING + XS + 4 + 3, 2, HEAD), F32),
+            pltpu.VMEM((RING + NEAR + 3, 2, HEAD), F32),
             pltpu.SemaphoreType.DMA((4,)),
             pltpu.SemaphoreType.DMA((2, 2, heads)),
             pltpu.SemaphoreType.DMA((2, 2, heads)),
             pltpu.SemaphoreType.DMA((2, 2, heads)),
             pltpu.SemaphoreType.DMA((2, 2, heads)),
-            pltpu.SemaphoreType.DMA((RING + XS + 4 + 3,)),
-            pltpu.SemaphoreType.DMA((RING + XS + 4 + 3,)),
+            pltpu.SemaphoreType.DMA((RING + NEAR + 3,)),
+            pltpu.SemaphoreType.DMA((RING + NEAR + 3,)),
             pltpu.SemaphoreType.DMA((3,)),
             pltpu.SemaphoreType.REGULAR,
         ],

time: 89.2 us -> 88.3 us (0.990)
  the two profiles are of different devices: /device:TPU:7 before, /device:TPU:1 now
where the time goes in v4:
time: 88.3 us; the launch traced here: 87.1 us
  Pallas kernels  86.4 us (98%)
    pallas_call x1, Pallas kernels, on_device(): pl.pallas_call(functools.partial(kernel, devices, docs, heads, group), ou...  83.7 us
    pallas_call x1, Pallas kernels, on_device(): pl.pallas_call(finish, out_shape=(jax.ShapeDtypeStruct(query_raw.shape, B...  2.69 us

profile of v4, /device:TPU:1, one launch (start us, length us, event | category | flops | bytes accessed | tf_op | source)
XLA Modules:
  0.0 87.1 jit_solution(2346445999923035462)
XLA Ops:
  0.6 83.7 %shard_map.119 = (bf16[128,2048]{1,0:T(8,128)(2,1)}, bf16[128,1024]{1,0:T(8,128)(2,1)}, bf16[128,1024]{1,0:T(8,128)(2,1)}, f32[2,128]{1,0:T(2,128)}) custom-call(s32[1,192]{1,0:T(1,128)} %bitcast.5, f32[1,128]{1,0:T(1,128)} %constant.2.clone.freq_ref, f32[1,128]{1,0:T(1,128)} %bitcast.6, f32[1,128]{1,0:T(1,128)} %bitcast.7, bf16[128,2048]{1,0:T(8,128)(2,1)} %q_hbm.1, ...), custom_call_target="tpu_custom_call" | custom-call | tf_op jit(solution)/shard_map/pallas_call | solution.py:406
  84.4 2.7 %shard_map.120 = (bf16[128,2048]{1,0:T(8,128)(2,1)}, bf16[128,1024]{1,0:T(8,128)(2,1)}, bf16[128,1024]{1,0:T(8,128)(2,1)}, f32[1,128]{1,0:T(1,128)}, f32[1,128]{1,0:T(1,128)}) custom-call(bf16[128,2048]{1,0:T(8,128)(2,1)} %get-tuple-element.14.dq_in, bf16[128,1024]{1,0:T(8,128)(2,1)} %get-tuple-element.15.dk_in, bf16[128,1024]{1,0:T(8,128)(2,1)} %get-tuple-element.16.dv_in, ...), custom_call_target="tpu_custom_call" | custom-call | tf_op jit(solution)/shard_map/pallas_call | solution.py:448
